TPU v7x, 32 devices: a whole 2x2x4 slice. The times are simulated.
32 devices in a mesh: groups: 2 (over y), tile: 4 (over z), chan: 2 (over x), tm: 2 (over core).
Axes of the slice: x: 2, y: 2, z: 4, core: 2. Of those that a mesh axis runs over, the one named last changes fastest.
Arguments:
- latents: bfloat16 [8, 32, 576], P('tm', 'groups', 'tile'), parts along dimension 1, may hold values from -6 to 6
- tile_order: int32 [8], P('groups'), parts along dimension 0, may hold values from 0 to 3, each once
- w_in: bfloat16 [27, 16, 512], P(None, None, 'chan'), may hold values from -0.3125 to 0.3125
- gain_in: float32 [512], P('chan'), may hold values from 0.25 to 1.75
- shift_in: float32 [512], P('chan'), may hold values from -3 to 3
- w_mid: bfloat16 [27, 512, 512], P(None, None, 'chan'), may hold values from -0.0546875 to 0.0546875
- gain_mid: float32 [512], P('chan'), may hold values from 0.25 to 1.75
- shift_mid: float32 [512], P('chan'), may hold values from -3 to 3
- w_out: bfloat16 [3, 512], P(None, 'chan'), may hold values from -0.25 to 0.25
- blend_weight: float32 [8, 256], P('groups'), parts along dimension 0, may hold values from 0.25 to 4
Outputs:
- decoded: float32 [8, 6, 576], P('tm', 'groups', 'tile'), parts along dimension 1
There are 2 independent parts, one for each index of `groups`. A program takes and returns all parts, laid end to end along the dimension named above; an argument that names none is the same for every part. Nothing has to cross between parts.
Inputs may be any that keep to these rules, and one draw needn't show every extreme that they name: `tile_order`: each image block is held by exactly one latent block.
All inputs are finite; a program needn't handle non-finite values.
Results may differ from a plain program's by a relative error of at most 0.0037.
Values may be sent and summed in bfloat16 or wider, within the bound.
A program may use at most 64 MiB of HBM per device.

v0:
```python
import jax
import jax.numpy as jnp
from jax import lax
from jax.sharding import PartitionSpec as P

CH = 512
GROUPS = 32
TSIDE = 16
STRIDE = 12
GRID_X = 4
EPSILON = 1e-06


def shifted(value, axis, steps):
    count = lax.axis_size(axis)
    leading, last = (max(0, -steps), min(count, count - steps))
    return lax.ppermute(value, axis, [(source, source + steps) for source in range(leading, last)])


def window_index(tile_id, tiles):
    slots = jnp.arange(TSIDE * TSIDE, dtype=jnp.int32)
    row = tile_id // GRID_X * STRIDE + slots // TSIDE
    col = tile_id % GRID_X * STRIDE + slots % TSIDE
    valid = (row < tiles // GRID_X * STRIDE) & (col < GRID_X * STRIDE)
    block = row // STRIDE * GRID_X + col // STRIDE
    index = block * (STRIDE * STRIDE) + row % STRIDE * STRIDE + col % STRIDE
    return (jnp.where(valid, index, 0), valid)


def causal_conv(extended, weights, frames, side):
    pixels = side * side
    rows = jnp.arange(pixels, dtype=jnp.int32) // side
    cols = jnp.arange(pixels, dtype=jnp.int32) % side
    total = jnp.zeros((frames, weights.shape[2], pixels), jnp.float32)
    for depth in range(3):
        window = extended[depth : depth + frames]
        for down in range(3):
            for across in range(3):
                offset = (down - 1) * side + (across - 1)
                inside = (
                    (rows + down - 1 >= 0)
                    & (rows + down - 1 < side)
                    & (cols + across - 1 >= 0)
                    & (cols + across - 1 < side)
                )
                moved = jnp.roll(window, -offset, axis=2)
                moved = jnp.where(inside[None, None, :], moved, jnp.zeros_like(moved))
                total = total + jnp.einsum(
                    "fcp,co->fop",
                    moved,
                    weights[9 * depth + 3 * down + across],
                    preferred_element_type=jnp.float32,
                )
    return total


def with_history(values):
    frames = values.shape[0]
    earlier = shifted(values[frames - 2 :], "tm", 1)
    return jnp.concatenate([earlier, values], axis=0)


def normalize(values, gain, shift, total_frames):
    frames, chans, pixels = values.shape
    width = CH // GROUPS
    grouped = values.reshape(frames, chans // width, width, pixels)
    sums = jnp.sum(grouped, axis=(0, 2, 3))
    squares = jnp.sum(grouped * grouped, axis=(0, 2, 3))
    sums, squares = lax.psum((sums, squares), "tm")
    count = total_frames * width * pixels
    mean = sums / count
    variance = squares / count - mean * mean
    scale = lax.rsqrt(variance + EPSILON)
    normed = (grouped - mean[None, :, None, None]) * scale[None, :, None, None]
    normed = normed.reshape(frames, chans, pixels) * gain[None, :, None] + shift[None, :, None]
    return jax.nn.silu(normed).astype(jnp.bfloat16)


def spread(color, weight, index, total_pixels):
    numer = (
        jnp.zeros((color.shape[0], 3, total_pixels), jnp.float32)
        .at[:, :, index]
        .add(color * weight[None, None, :])
    )
    denom = jnp.zeros((total_pixels,), jnp.float32).at[index].add(weight)
    return (numer, denom)


def route_owned(numer, denom, tile_id, own):
    frames = numer.shape[0]
    margin = (GRID_X + 1) * own
    numer_wide = jnp.concatenate([numer, jnp.zeros((frames, 3, margin), jnp.float32)], axis=2)
    denom_wide = jnp.concatenate([denom, jnp.zeros((margin,), jnp.float32)], axis=0)
    first_pixel = tile_id * own

    def block_at(offset):
        start_pixel = first_pixel + offset * own
        return (
            lax.dynamic_slice_in_dim(numer_wide, start_pixel, own, 2),
            lax.dynamic_slice_in_dim(denom_wide, start_pixel, own, 0),
        )

    owned_numer, owned_denom = block_at(0)
    for offset in (1, GRID_X, GRID_X + 1):
        piece_numer, piece_denom = block_at(offset)
        got_numer, got_denom = shifted((piece_numer, piece_denom), "tile", offset)
        owned_numer = owned_numer + got_numer
        owned_denom = owned_denom + got_denom
    return (owned_numer, owned_denom)


def body(
    latents, tile_order, w_in, gain_in, shift_in, w_mid, gain_mid, shift_mid, w_out, blend_weight
):
    frames = latents.shape[0]
    total_frames = frames * lax.axis_size("tm")
    tiles = tile_order.shape[0]
    own = STRIDE * STRIDE
    total_pixels = tiles * own
    tile_id = lax.axis_index("tile")
    index, valid = window_index(tile_id, tiles)
    whole = lax.all_gather(latents, "tile", axis=2, tiled=True)
    blocks = whole.reshape(frames, whole.shape[1], tiles, own)
    image = (
        jnp.zeros_like(blocks)
        .at[:, :, tile_order]
        .set(blocks)
        .reshape(frames, whole.shape[1], total_pixels)
    )
    window = jnp.where(
        valid[None, None, :], jnp.take(image, index, axis=2), jnp.zeros((), jnp.bfloat16)
    )
    first = causal_conv(with_history(window), w_in, frames, TSIDE)
    hidden = normalize(first, gain_in, shift_in, total_frames)
    second = causal_conv(
        lax.all_gather(with_history(hidden), "chan", axis=1, tiled=True), w_mid, frames, TSIDE
    )
    upper = normalize(second, gain_mid, shift_mid, total_frames)
    color = jnp.einsum("oc,fcp->fop", w_out, upper, preferred_element_type=jnp.float32)
    weight = jnp.where(valid, blend_weight[tile_id], jnp.float32(0.0))
    numer, denom = spread(color, weight, index, total_pixels)
    numer, denom = route_owned(numer, denom, tile_id, own)
    numer = lax.psum(numer, "chan")
    return numer / denom[None, None, :]


def solution(mesh):
    placed = (
        P("tm", "groups", "tile"),
        P("groups"),
        P(None, None, "chan"),
        P("chan"),
        P("chan"),
        P(None, None, "chan"),
        P("chan"),
        P("chan"),
        P(None, "chan"),
        P("groups", None),
    )
    return jax.shard_map(
        body, mesh=mesh, in_specs=placed, out_specs=P("tm", "groups", "tile"), check_vma=False
    )
```

profile of v0, /device:TPU:0, one launch (start us, length us, event | category | flops | bytes accessed | tf_op | source)
XLA Modules:
  0.0 141.7 jit_solution(11770328538480830236)
XLA Ops:
  6.6 1.0 copy.204
  7.6 18.3 %all_gather.6 = bf16[4,16,576]{1,0,2:T(4,128)(2,1)S(1)} all-gather(bf16[4,16,144]{1,0,2:T(4,128)(2,1)S(1)} %copy.204), channel_id=1, replica_groups=mesh['groups'=2,'tile'=4,'chan'=2,'tm'=2] {'tile'}, dimensions={2}, use_global_device_ids=true | all-gather | bytes 92160 | tf_op jit(solution)/shard_map/all_gather | solution.py:122
  26.2 0.7 compare_select_fusion.2
  26.9 0.7 scatter_fusion
  27.9 1.0 gather_fusion
  29.1 1.3 collective-permute-start
  30.5 0.7 collective-permute-done
  43.4 2.5 %all-reduce.3 = (f32[16]{0:T(128)S(1)}, f32[16]{0:T(128)S(1)}) all-reduce(f32[16]{0:T(128)S(1)} %reduce_sum.54, f32[16]{0:T(128)S(1)} %reduce_sum.51), channel_id=1, replica_groups=mesh['groups'=2,'tile'=4,'chan'=2,'tm'=2] {'tm'}, use_global_device_ids=true, to_apply=%region_6.7 | all-reduce | flops 32 | bytes 256 | tf_op jit(solution)/shard_map/psum | solution.py:69
  46.6 2.3 %collective-permute-start.1 = (bf16[2,256,256]{1,2,0:T(8,128)(2,1)S(1)}, bf16[2,256,256]{1,2,0:T(8,128)(2,1)S(1)}, u32[]{:S(2)}, u32[]{:S(2)}) collective-permute-start(bf16[2,256,256]{1,2,0:T(8,128)(2,1)S(1)} %slice.825), channel_id=1, source_target_pairs={{0,1},{2,3},{4,5},{6,7},{8,9},{10,11},{12,13},{14,15},{16,17},{18,... | collective-permute-start | bytes 786440 | tf_op jit(solution)/shard_map/ppermute | solution.py:17
  48.9 1.1 collective-permute-done.1
  50.0 0.9 pad_maximum_fusion
  51.0 2.3 %scatter_custom_fusion.2 = f32[576]{0:T(1024)S(1)} fusion(s32[256]{0:T(256)S(1)} %bitcast.322, f32[256]{0:T(256)S(1)} %broadcast_select_fusion, f32[]{:T(128)} %constant.166.clone.1), kind=kCustom, calls=%fused_computation.579 | custom fusion | flops 256 | bytes 2308 | tf_op jit(solution)/shard_map/scatter-add | solution.py:85
  53.4 3.4 %collective-permute-start.5 = (f32[144]{0:T(256)S(1)}, f32[144]{0:T(256)S(1)}, u32[]{:S(2)}, u32[]{:S(2)}) collective-permute-start(f32[144]{0:T(256)S(1)} %get-tuple-element.115), channel_id=1, source_target_pairs={{0,4},{4,8},{8,12},{1,5},{5,9},{9,13},{2,6},{6,10},{10,14},{3,7},{... | collective-permute-start | bytes 1736 | tf_op jit(solution)/shard_map/ppermute | solution.py:17
  56.9 0.7 collective-permute-start.6
  57.5 0.8 collective-permute-start.7
  58.4 21.1 %all-gather.2.cloned.1.call-done = bf16[6,512,256]{1,2,0:T(8,128)(2,1)} async-done(((bf16[6,256,256]{1,2,0:T(8,128)(2,1)}), bf16[6,512,256]{1,2,0:T(8,128)(2,1)}) %all-gather.2.cloned.1.call-update) | async-done | bytes 1572880 | tf_op jit(solution)/shard_map/all_gather | solution.py:136
  79.5 4.2 %fusion.506 = (bf16[4,512,239]{1,2,0:T(8,128)(2,1)S(1)}, bf16[4,512,239]{1,2,0:T(8,128)(2,1)S(1)}, bf16[4,512,239]{1,2,0:T(8,128)(2,1)S(1)}, bf16[4,512,239]{1,2...) fusion(bf16[6,512,256]{1,2,0:T(8,128)(2,1)} %all-gather.2.cloned.1.call-done), kind=kLoop, calls=%fused_computation.741 | loop fusion | bytes 11747328 | tf_op jit(solution)/shard_map/jit(_roll_static)/slice | solution.py:46
  83.8 1.4 %fusion.23 = f32[4,256,256]{2,1,0:T(8,128)S(1)} fusion(bf16[4,512,239]{1,2,0:T(8,128)(2,1)S(1)} %get-tuple-element.30, bf16[4,512,17]{1,2,0:T(8,128)(2,1)S(1)} %get-tuple-element.36, pred[256]{0:T(512)(128)(4,1)S(1)} %and_and_fusion.8, bf16[27,512,256]{2,1,0:T(8,128)(2,1)} %param.15), kind=kOutput, calls=%fused_computation.84 | convolution fusion | flops 271056896 | bytes 2359552 | tf_op jit(solution)/shard_map/fcp,co->fop/dot_general | solution.py:48
  85.2 1.4 %convolution_bitcast_fusion.8 = f32[4,256,256]{1,2,0:T(8,128)S(1)} fusion(bf16[4,512,239]{1,2,0:T(8,128)(2,1)S(1)} %get-tuple-element.27, bf16[4,512,17]{1,2,0:T(8,128)(2,1)S(1)} %get-tuple-element.33, pred[256]{0:T(512)(128)(4,1)S(1)} %and_and_fusion.8, bf16[27,512,256]{2,1,0:T(8,128)(2,1)} %param.15), kind=kOutput, calls=%fused_computation.12 | convolution fusion | flops 271056896 | bytes 2359552 | tf_op jit(solution)/shard_map/fcp,co->fop/dot_general | solution.py:48
  86.7 0.7 fusion.508
  87.4 1.4 %convolution_bitcast_fusion.7 = f32[4,256,256]{1,2,0:T(8,128)S(1)} fusion(bf16[4,512,240]{1,2,0:T(8,128)(2,1)S(1)} %get-tuple-element.39, bf16[4,512,16]{1,2,0:T(8,128)(2,1)S(1)} %get-tuple-element.45, pred[256]{0:T(512)(128)(4,1)S(1)} %get-tuple-element.131, bf16[27,512,256]{2,1,0:T(8,128)(2,1)} %param.15), kind=kOutput, calls=%fused_computation.11 | convolution fusion | flops 271056896 | bytes 2359552 | tf_op jit(solution)/shard_map/fcp,co->fop/dot_general | solution.py:48
  88.8 0.7 fusion.510
  89.6 1.5 %convolution_bitcast_fusion.6 = f32[4,256,256]{1,2,0:T(8,128)S(1)} fusion(bf16[4,512,241]{1,2,0:T(8,128)(2,1)S(1)} %get-tuple-element.51, bf16[4,512,15]{1,2,0:T(8,128)(2,1)S(1)} %get-tuple-element.57, pred[256]{0:T(512)(128)(4,1)S(1)} %get-tuple-element.130, bf16[27,512,256]{2,1,0:T(8,128)(2,1)} %param.15), kind=kOutput, calls=%fused_computation.10 | convolution fusion | flops 271056896 | bytes 2359552 | tf_op jit(solution)/shard_map/fcp,co->fop/dot_general | solution.py:48
  91.0 0.8 fusion.504
  91.9 1.4 %convolution_bitcast_fusion.5 = f32[4,256,256]{1,2,0:T(8,128)S(1)} fusion(bf16[4,512,255]{1,2,0:T(8,128)(2,1)S(1)} %get-tuple-element.14, bf16[4,512,1]{1,2,0:T(2,128)(2,1)S(1)} %get-tuple-element.20, pred[256]{0:T(512)(128)(4,1)S(1)} %get-tuple-element.129, bf16[27,512,256]{2,1,0:T(8,128)(2,1)} %param.15), kind=kOutput, calls=%fused_computation.9 | convolution fusion | flops 271056896 | bytes 2359552 | tf_op jit(solution)/shard_map/fcp,co->fop/dot_general | solution.py:48
  93.4 1.6 %convolution_bitcast_fusion.2 = f32[4,256,256]{1,2,0:T(8,128)S(1)} fusion(bf16[4,512,15]{1,2,0:T(8,128)(2,1)S(1)} %get-tuple-element.56, bf16[4,512,241]{1,2,0:T(8,128)(2,1)S(1)} %get-tuple-element.50, pred[256]{0:T(512)(128)(4,1)S(1)} %get-tuple-element.126, bf16[27,512,256]{2,1,0:T(8,128)(2,1)} %param.15), kind=kOutput, calls=%fused_computation.6 | convolution fusion | flops 271056896 | bytes 2359552 | tf_op jit(solution)/shard_map/fcp,co->fop/dot_general | solution.py:48
  95.0 1.4 %convolution_bitcast_fusion.1 = f32[4,256,256]{1,2,0:T(8,128)S(1)} fusion(bf16[4,512,16]{1,2,0:T(8,128)(2,1)S(1)} %get-tuple-element.44, bf16[4,512,240]{1,2,0:T(8,128)(2,1)S(1)} %get-tuple-element.38, pred[256]{0:T(512)(128)(4,1)S(1)} %get-tuple-element.125, bf16[27,512,256]{2,1,0:T(8,128)(2,1)} %param.15), kind=kOutput, calls=%fused_computation.5 | convolution fusion | flops 271056896 | bytes 2359552 | tf_op jit(solution)/shard_map/fcp,co->fop/dot_general | solution.py:48
  96.4 1.6 %convolution_bitcast_fusion = f32[4,256,256]{1,2,0:T(8,128)S(1)} fusion(bf16[4,512,17]{1,2,0:T(8,128)(2,1)S(1)} %get-tuple-element.32, bf16[4,512,239]{1,2,0:T(8,128)(2,1)S(1)} %get-tuple-element.26, pred[256]{0:T(512)(128)(4,1)S(1)} %get-tuple-element.124, bf16[27,512,256]{2,1,0:T(8,128)(2,1)} %param.15), kind=kOutput, calls=%fused_computation.4 | convolution fusion | flops 271056896 | bytes 2359552 | tf_op jit(solution)/shard_map/fcp,co->fop/dot_general | solution.py:48
  98.0 1.5 %convolution_add_fusion.31 = f32[4,256,256]{2,1,0:T(8,128)S(1)} fusion(f32[4,256,256]{2,1,0:T(8,128)S(1)} %fusion.23, bf16[4,512,240]{1,2,0:T(8,128)(2,1)S(1)} %get-tuple-element.42, bf16[4,512,16]{1,2,0:T(8,128)(2,1)S(1)} %get-tuple-element.48, pred[256]{0:T(512)(128)(4,1)S(1)} %get-tuple-element.131, bf16[27,512,256]{2,1,0:T(8,128)(2,1)} %param.15), kind=kOutput, calls=%fused_computation.77 | convolution fusion | flops 271319040 | bytes 3408128 | tf_op jit(solution)/shard_map/fcp,co->fop/dot_general | solution.py:48
  99.5 0.5 convolution_add_fusion.30
  100.0 0.5 convolution_add_fusion.29
  102.0 0.5 convolution_add_fusion.25
  102.5 0.5 convolution_add_fusion.24
  103.0 0.5 convolution_add_fusion.23
  104.0 0.5 convolution_add_fusion.21
  104.5 0.5 convolution_add_fusion.20
  105.5 0.5 convolution_add_fusion.18
  106.0 0.7 convolution_add_fusion.17
  106.7 0.5 fusion.21
  107.7 0.6 fusion.16
  108.4 0.6 fusion.502
  109.4 2.5 %all-reduce.2 = (f32[16]{0:T(128)S(1)}, f32[16]{0:T(128)S(1)}) all-reduce(f32[16]{0:T(128)S(1)} %reduce_sum.75, f32[16]{0:T(128)S(1)} %reduce_sum.72), channel_id=1, replica_groups=mesh['groups'=2,'tile'=4,'chan'=2,'tm'=2] {'tm'}, use_global_device_ids=true, to_apply=%region_12.13 | all-reduce | flops 32 | bytes 256 | tf_op jit(solution)/shard_map/psum | solution.py:69
  113.1 8.5 %scatter_fusion.1 = f32[4,3,576]{1,0,2:T(4,128)S(1)} fusion(f32[4,3,576]{1,0,2:T(4,128)S(1)} %broadcast_in_dim.385, s32[256]{0:T(256)S(1)} %bitcast.323, f32[256,4,3]{2,1,0:T(4,128)S(1)} %copy.210), kind=kCustom, calls=%fused_computation.2 | custom fusion | flops 3072 | bytes 37888 | tf_op jit(solution)/shard_map/scatter-add | solution.py:83
  122.2 3.4 %collective-permute-start.2 = (f32[4,3,144]{2,0,1:T(4,128)S(1)}, f32[4,3,144]{2,0,1:T(4,128)S(1)}, u32[]{:S(2)}, u32[]{:S(2)}) collective-permute-start(f32[4,3,144]{2,0,1:T(4,128)S(1)} %get-tuple-element.112), channel_id=1, source_target_pairs={{0,4},{4,8},{8,12},{1,5},{5,9},{9,13},{2,6},{6,10},{10,14},{3,7},{... | collective-permute-start | bytes 20744 | tf_op jit(solution)/shard_map/ppermute | solution.py:17
  125.6 0.7 collective-permute-start.3
  126.2 0.7 collective-permute-start.4
  127.1 7.1 %psum.39 = f32[4,3,144]{2,0,1:T(4,128)S(1)} all-reduce(f32[4,3,144]{2,0,1:T(4,128)S(1)} %fusion.326), channel_id=1, replica_groups=mesh['groups'=2,'tile'=4,'chan'=2,'tm'=2] {'chan'}, use_global_device_ids=true, to_apply=%region_14.15 | all-reduce | flops 1728 | bytes 13824 | tf_op jit(solution)/shard_map/psum | solution.py:143
  134.2 0.6 broadcast_divide_fusion
  (120 shorter events, 19.1 us)
Async XLA Ops:
  6.5 44.4 %copy-start = (f32[4,256]{1,0:T(4,128)S(1)}, f32[4,256]{1,0:T(4,128)}, u32[]{:S(2)}) copy-start(f32[4,256]{1,0:T(4,128)} %param.19) | copy-start | bytes 12292
  6.5 24.9 %copy-start.3 = (bf16[27,16,256]{2,1,0:T(8,128)(2,1)S(1)}, bf16[27,16,256]{2,1,0:T(8,128)(2,1)}, u32[]{:S(2)}) copy-start(bf16[27,16,256]{2,1,0:T(8,128)(2,1)} %param.12) | copy-start | bytes 663556
  6.5 72.9 %all-gather.2.cloned.1.call-start = ((), (), s32[]{:S(2)}) async-start(), calls=%async_computation | async-start | bytes 2359296 | tf_op jit(solution)/shard_map/all_gather | solution.py:136
  29.1 2.1 %collective-permute-start = (bf16[2,16,256]{2,1,0:T(8,128)(2,1)S(1)}, bf16[2,16,256]{2,1,0:T(8,128)(2,1)S(1)}, u32[]{:S(2)}, u32[]{:S(2)}) collective-permute-start(bf16[2,16,256]{2,1,0:T(8,128)(2,1)S(1)} %slice.742), channel_id=1, source_target_pairs={{0,1},{2,3},{4,5},{6,7},{8,9},{10,11},{12,13},{14,15},{16,17},{18,... | collective-permute-start | bytes 49160 | tf_op jit(solution)/shard_map/ppermute | solution.py:17
  42.2 4.1 %copy-start.4 = (f32[256]{0:T(256)S(1)}, f32[256]{0:T(256)}, u32[]{:S(2)}) copy-start(f32[256]{0:T(256)} %param.14) | copy-start | bytes 3076
  42.2 4.0 %copy-start.5 = (f32[256]{0:T(256)S(1)}, f32[256]{0:T(256)}, u32[]{:S(2)}) copy-start(f32[256]{0:T(256)} %param.13) | copy-start | bytes 3076
  46.6 3.4 %collective-permute-start.1 = (bf16[2,256,256]{1,2,0:T(8,128)(2,1)S(1)}, bf16[2,256,256]{1,2,0:T(8,128)(2,1)S(1)}, u32[]{:S(2)}, u32[]{:S(2)}) collective-permute-start(bf16[2,256,256]{1,2,0:T(8,128)(2,1)S(1)} %slice.825), channel_id=1, source_target_pairs={{0,1},{2,3},{4,5},{6,7},{8,9},{10,11},{12,13},{14,15},{16,17},{18,... | collective-permute-start | bytes 786440 | tf_op jit(solution)/shard_map/ppermute | solution.py:17
  53.4 72.8 %collective-permute-start.5 = (f32[144]{0:T(256)S(1)}, f32[144]{0:T(256)S(1)}, u32[]{:S(2)}, u32[]{:S(2)}) collective-permute-start(f32[144]{0:T(256)S(1)} %get-tuple-element.115), channel_id=1, source_target_pairs={{0,4},{4,8},{8,12},{1,5},{5,9},{9,13},{2,6},{6,10},{10,14},{3,7},{... | collective-permute-start | bytes 1736 | tf_op jit(solution)/shard_map/ppermute | solution.py:17
  56.9 70.0 %collective-permute-start.6 = (f32[144]{0:T(256)S(1)}, f32[144]{0:T(256)S(1)}, u32[]{:S(2)}, u32[]{:S(2)}) collective-permute-start(f32[144]{0:T(256)S(1)} %get-tuple-element.116), channel_id=1, source_target_pairs={} | collective-permute-start | bytes 1736 | tf_op jit(solution)/shard_map/ppermute | solution.py:17
  57.5 69.4 %collective-permute-start.7 = (f32[144]{0:T(256)S(1)}, f32[144]{0:T(256)S(1)}, u32[]{:S(2)}, u32[]{:S(2)}) collective-permute-start(f32[144]{0:T(256)S(1)} %get-tuple-element.117), channel_id=1, source_target_pairs={} | collective-permute-start | bytes 1736 | tf_op jit(solution)/shard_map/ppermute | solution.py:17
  79.5 4.2 %copy-start.2 = (bf16[6,512,256]{1,2,0:T(8,128)(2,1)S(1)}, bf16[6,512,256]{1,2,0:T(8,128)(2,1)}, u32[]{:S(2)}) copy-start(bf16[6,512,256]{1,2,0:T(8,128)(2,1)} %all-gather.2.cloned.1.call-done) | copy-start | bytes 4718596
  93.4 6.1 %slice-start = ((s8[7077888]{0:T(1024)(128)(4,1)}), s8[4194304]{0:T(1024)(128)(4,1)S(1)}, s32[]{:S(2)}) async-start(s8[7077888]{0:T(1024)(128)(4,1)} %bitcast.319), calls=%async_computation.1 | async-start | bytes 8388608
  96.4 3.1 %slice-start.1 = ((s8[7077888]{0:T(1024)(128)(4,1)}), s8[2883584]{0:T(1024)(128)(4,1)S(1)}, s32[]{:S(2)}) async-start(s8[7077888]{0:T(1024)(128)(4,1)} %bitcast.319), calls=%async_computation.2 | async-start | bytes 5767168
  108.4 3.8 %copy-start.6 = (bf16[3,256]{1,0:T(4,128)(2,1)S(1)}, bf16[3,256]{1,0:T(4,128)(2,1)}, u32[]{:S(2)}) copy-start(bf16[3,256]{1,0:T(4,128)(2,1)} %param.18) | copy-start | bytes 4612
  108.4 3.8 %copy-start.7 = (f32[256]{0:T(256)S(1)}, f32[256]{0:T(256)}, u32[]{:S(2)}) copy-start(f32[256]{0:T(256)} %param.17) | copy-start | bytes 3076
  108.4 3.8 %copy-start.8 = (f32[256]{0:T(256)S(1)}, f32[256]{0:T(256)}, u32[]{:S(2)}) copy-start(f32[256]{0:T(256)} %param.16) | copy-start | bytes 3076
  112.7 22.2 %copy-start.1 = (f32[4,256]{1,0:T(4,128)S(1)}, f32[4,256]{1,0:T(4,128)}, u32[]{:S(2)}) copy-start(f32[4,256]{1,0:T(4,128)} %param.19) | copy-start | bytes 12292
  122.2 4.8 %collective-permute-start.2 = (f32[4,3,144]{2,0,1:T(4,128)S(1)}, f32[4,3,144]{2,0,1:T(4,128)S(1)}, u32[]{:S(2)}, u32[]{:S(2)}) collective-permute-start(f32[4,3,144]{2,0,1:T(4,128)S(1)} %get-tuple-element.112), channel_id=1, source_target_pairs={{0,4},{4,8},{8,12},{1,5},{5,9},{9,13},{2,6},{6,10},{10,14},{3,7},{... | collective-permute-start | bytes 20744 | tf_op jit(solution)/shard_map/ppermute | solution.py:17
  125.6 1.4 %collective-permute-start.3 = (f32[4,3,144]{2,0,1:T(4,128)S(1)}, f32[4,3,144]{2,0,1:T(4,128)S(1)}, u32[]{:S(2)}, u32[]{:S(2)}) collective-permute-start(f32[4,3,144]{2,0,1:T(4,128)S(1)} %get-tuple-element.113), channel_id=1, source_target_pairs={} | collective-permute-start | bytes 20744 | tf_op jit(solution)/shard_map/ppermute | solution.py:17
  126.2 0.8 collective-permute-start.4
Sparse Core Ops, SparseCore 0:
  51.1 28.3 all-gather.1
where the time goes:
time: 142 us
  matrix products  33.9 us (24%)
  blocking collectives  30.3 us (21%)
  waiting for transfers between devices  23 us (16%)
  other arithmetic  14.9 us (10%)
  between operations  14.3 us (10%)
  starting transfers between devices  13.2 us (9%)
  local copies, waits for them, and re-layouts  12.1 us (9%)
    dot_general x54, matrix products, causal_conv(): jnp.einsum('fcp,co->fop', moved, weights[9 * depth + 3 * down + across],...  33.5 us
    all_gather x1, waiting for transfers between devices, body(): lax.all_gather(with_history(hidden), 'chan', axis=1, tiled=True)  21.1 us
    all_gather x1, blocking collectives, body(): whole = lax.all_gather(latents, 'tile', axis=2, tiled=True)  18.3 us
    ppermute x8, starting transfers between devices, shifted(): lax.ppermute(value, axis, [(source, source + steps) for source in range(l...  13.2 us
    scatter-add x1, other arithmetic, spread(): numer = jnp.zeros((color.shape[0], 3, total_pixels), jnp.float32).at[:, :...  8.52 us
    psum x1, blocking collectives, body(): numer = lax.psum(numer, 'chan')  7.13 us
    slice x8, local copies, waits for them, and re-layouts, causal_conv(): moved = jnp.roll(window, -offset, axis=2)  6.55 us
    psum x2, blocking collectives, normalize(): sums, squares = lax.psum((sums, squares), 'tm')  4.95 us
  transfers between devices with their start and end apart: 9, of which 3 were waited for; matrix products, arithmetic and copies ran while one was open for 30% of the time, Pallas kernels for 0%

commit v1 on v0

--- a/solution.py
+++ b/solution.py
@@ -1,3 +1,4 @@
+import functools
 import jax
 import jax.numpy as jnp
 from jax import lax
@@ -9,6 +10,14 @@
 STRIDE = 12
 GRID_X = 4
 EPSILON = 1e-06
+
+
+def _name_yards(vals, which_axis):
+    taken_in = lax.ppermute(vals, which_axis, [(0, 1), (1, 0)])
+    return vals + taken_in
+
+
+use_sizes_over_axis = functools.partial(_name_yards, which_axis="chan")
 
 
 def shifted(value, axis, steps):
@@ -140,7 +149,7 @@
     weight = jnp.where(valid, blend_weight[tile_id], jnp.float32(0.0))
     numer, denom = spread(color, weight, index, total_pixels)
     numer, denom = route_owned(numer, denom, tile_id, own)
-    numer = lax.psum(numer, "chan")
+    numer = use_sizes_over_axis(numer)
     return numer / denom[None, None, :]
 
 

time: 142 us -> 150 us (1.056)
  waiting for transfers between devices: 23 us -> 36.5 us
  blocking collectives: 30.3 us -> 23.2 us
    ppermute x0 -> x1, waiting for transfers between devices: none -> 7.56 us  [_name_yards(): taken_in = lax.ppermute(vals, which_axis, [(0, 1), (1, 0)])]
    psum x1 -> x0, blocking collectives: 7.13 us -> none  [body(): numer = lax.psum(numer, 'chan')]
    all_gather x1, waiting for transfers between devices: 21.1 us -> 26 us  [body(): lax.all_gather(with_history(hidden), 'chan', axis=1, tiled=True)]
  transfers between devices with their start and end apart: 9 -> 10, of which waited for: 3 -> 5; matrix products, arithmetic and copies ran while one was open for 30% -> 2% of each run, Pallas kernels for 0% -> 0%
where the time goes in v1:
time: 150 us; the launch traced here: 149 us
  waiting for transfers between devices  36.5 us (24%)
  matrix products  33.8 us (23%)
  blocking collectives  23.2 us (15%)
  other arithmetic  14.9 us (10%)
  between operations  14.3 us (10%)
  starting transfers between devices  13.6 us (9%)
  local copies, waits for them, and re-layouts  13.1 us (9%)
    dot_general x54, matrix products, causal_conv(): jnp.einsum('fcp,co->fop', moved, weights[9 * depth + 3 * down + across],...  33.3 us
    all_gather x1, waiting for transfers between devices, body(): lax.all_gather(with_history(hidden), 'chan', axis=1, tiled=True)  26 us
    all_gather x1, blocking collectives, body(): whole = lax.all_gather(latents, 'tile', axis=2, tiled=True)  18.3 us
    ppermute x8, starting transfers between devices, shifted(): lax.ppermute(value, axis, [(source, source + steps) for source in range(l...  13 us
    scatter-add x1, other arithmetic, spread(): numer = jnp.zeros((color.shape[0], 3, total_pixels), jnp.float32).at[:, :...  8.52 us
    ppermute x1, waiting for transfers between devices, _name_yards(): taken_in = lax.ppermute(vals, which_axis, [(0, 1), (1, 0)])  7.56 us
    slice x8, local copies, waits for them, and re-layouts, causal_conv(): moved = jnp.roll(window, -offset, axis=2)  6.65 us
    psum x2, blocking collectives, normalize(): sums, squares = lax.psum((sums, squares), 'tm')  4.95 us
  transfers between devices with their start and end apart: 10, of which 5 were waited for; matrix products, arithmetic and copies ran while one was open for 2% of the time, Pallas kernels for 0%

profile of v1, /device:TPU:0, one launch (start us, length us, event | category | flops | bytes accessed | tf_op | source)
XLA Modules:
  0.0 149.4 jit_solution(7941252291894022096)
XLA Ops:
  6.6 1.0 copy.204
  7.6 18.3 %all_gather.6 = bf16[4,16,576]{1,0,2:T(4,128)(2,1)S(1)} all-gather(bf16[4,16,144]{1,0,2:T(4,128)(2,1)S(1)} %copy.204), channel_id=1, replica_groups=mesh['groups'=2,'tile'=4,'chan'=2,'tm'=2] {'tile'}, dimensions={2}, use_global_device_ids=true | all-gather | bytes 92160 | tf_op jit(solution)/shard_map/all_gather | solution.py:131
  26.2 0.7 compare_select_fusion.2
  26.9 0.7 scatter_fusion
  27.9 1.0 gather_fusion
  29.1 1.3 collective-permute-start
  30.5 0.7 collective-permute-done
  43.4 2.5 %all-reduce.3 = (f32[16]{0:T(128)S(1)}, f32[16]{0:T(128)S(1)}) all-reduce(f32[16]{0:T(128)S(1)} %reduce_sum.54, f32[16]{0:T(128)S(1)} %reduce_sum.51), channel_id=1, replica_groups=mesh['groups'=2,'tile'=4,'chan'=2,'tm'=2] {'tm'}, use_global_device_ids=true, to_apply=%region_6.7 | all-reduce | flops 32 | bytes 256 | tf_op jit(solution)/shard_map/psum | solution.py:78
  46.6 2.3 %collective-permute-start.1 = (bf16[2,256,256]{1,2,0:T(8,128)(2,1)S(1)}, bf16[2,256,256]{1,2,0:T(8,128)(2,1)S(1)}, u32[]{:S(2)}, u32[]{:S(2)}) collective-permute-start(bf16[2,256,256]{1,2,0:T(8,128)(2,1)S(1)} %slice.825), channel_id=1, source_target_pairs={{0,1},{2,3},{4,5},{6,7},{8,9},{10,11},{12,13},{14,15},{16,17},{18,... | collective-permute-start | bytes 786440 | tf_op jit(solution)/shard_map/ppermute | solution.py:26
  48.9 1.1 collective-permute-done.1
  50.0 1.0 pad_maximum_fusion
  51.0 2.5 %scatter_custom_fusion.2 = f32[576]{0:T(1024)S(1)} fusion(s32[256]{0:T(256)S(1)} %bitcast.322, f32[256]{0:T(256)S(1)} %broadcast_select_fusion, f32[]{:T(128)} %constant.166.clone.1), kind=kCustom, calls=%fused_computation.579 | custom fusion | flops 256 | bytes 2308 | tf_op jit(solution)/shard_map/scatter-add | solution.py:94
  53.5 26.0 %all-gather.2.cloned.1.call-done = bf16[6,512,256]{1,2,0:T(8,128)(2,1)} async-done(((bf16[6,256,256]{1,2,0:T(8,128)(2,1)}), bf16[6,512,256]{1,2,0:T(8,128)(2,1)}) %all-gather.2.cloned.1.call-update) | async-done | bytes 1572880 | tf_op jit(solution)/shard_map/all_gather | solution.py:145
  79.5 4.3 %fusion.506 = (bf16[4,512,239]{1,2,0:T(8,128)(2,1)S(1)}, bf16[4,512,239]{1,2,0:T(8,128)(2,1)S(1)}, bf16[4,512,239]{1,2,0:T(8,128)(2,1)S(1)}, bf16[4,512,239]{1,2...) fusion(bf16[6,512,256]{1,2,0:T(8,128)(2,1)} %all-gather.2.cloned.1.call-done), kind=kLoop, calls=%fused_computation.741 | loop fusion | bytes 11747328 | tf_op jit(solution)/shard_map/jit(_roll_static)/slice | solution.py:55
  83.9 1.4 fusion.23
  85.4 1.4 convolution_bitcast_fusion.8
  86.8 0.7 fusion.508
  87.5 1.4 convolution_bitcast_fusion.7
  89.0 0.7 fusion.510
  89.7 1.4 convolution_bitcast_fusion.6
  91.1 0.8 fusion.504
  92.0 1.5 convolution_bitcast_fusion.5
  93.5 1.6 %convolution_bitcast_fusion.2 = f32[4,256,256]{1,2,0:T(8,128)S(1)} fusion(bf16[4,512,15]{1,2,0:T(8,128)(2,1)S(1)} %get-tuple-element.56, bf16[4,512,241]{1,2,0:T(8,128)(2,1)S(1)} %get-tuple-element.50, pred[256]{0:T(512)(128)(4,1)S(1)} %get-tuple-element.126, bf16[27,512,256]{2,1,0:T(8,128)(2,1)} %param.15), kind=kOutput, calls=%fused_computation.10 | convolution fusion | flops 271056896 | bytes 2359552 | tf_op jit(solution)/shard_map/fcp,co->fop/dot_general | solution.py:57
  95.1 1.4 convolution_bitcast_fusion.1
  96.5 1.6 %convolution_bitcast_fusion = f32[4,256,256]{1,2,0:T(8,128)S(1)} fusion(bf16[4,512,17]{1,2,0:T(8,128)(2,1)S(1)} %get-tuple-element.32, bf16[4,512,239]{1,2,0:T(8,128)(2,1)S(1)} %get-tuple-element.26, pred[256]{0:T(512)(128)(4,1)S(1)} %get-tuple-element.124, bf16[27,512,256]{2,1,0:T(8,128)(2,1)} %param.15), kind=kOutput, calls=%fused_computation.8 | convolution fusion | flops 271056896 | bytes 2359552 | tf_op jit(solution)/shard_map/fcp,co->fop/dot_general | solution.py:57
  98.1 1.4 convolution_add_fusion.31
  99.5 0.5 convolution_add_fusion.30
  100.1 0.5 convolution_add_fusion.29
  103.0 0.5 convolution_add_fusion.23
  104.0 0.5 convolution_add_fusion.21
  104.5 0.5 convolution_add_fusion.20
  106.0 0.7 convolution_add_fusion.17
  106.7 0.5 fusion.21
  107.7 0.6 fusion.16
  108.4 0.6 fusion.502
  109.4 2.5 %all-reduce.2 = (f32[16]{0:T(128)S(1)}, f32[16]{0:T(128)S(1)}) all-reduce(f32[16]{0:T(128)S(1)} %reduce_sum.75, f32[16]{0:T(128)S(1)} %reduce_sum.72), channel_id=1, replica_groups=mesh['groups'=2,'tile'=4,'chan'=2,'tm'=2] {'tm'}, use_global_device_ids=true, to_apply=%region_12.13 | all-reduce | flops 32 | bytes 256 | tf_op jit(solution)/shard_map/psum | solution.py:78
  113.1 8.5 %scatter_fusion.1 = f32[4,3,576]{1,0,2:T(4,128)S(1)} fusion(f32[4,3,576]{1,0,2:T(4,128)S(1)} %broadcast_in_dim.385, s32[256]{0:T(256)S(1)} %bitcast.323, f32[256,4,3]{2,1,0:T(4,128)S(1)} %copy.210), kind=kCustom, calls=%fused_computation.2 | custom fusion | flops 3072 | bytes 37888 | tf_op jit(solution)/shard_map/scatter-add | solution.py:92
  121.6 0.7 pad_dynamic-slice_fusion.2
  122.3 3.4 %collective-permute-start.2 = (f32[4,3,144]{1,0,2:T(4,128)S(1)}, f32[4,3,144]{1,0,2:T(4,128)S(1)}, u32[]{:S(2)}, u32[]{:S(2)}) collective-permute-start(f32[4,3,144]{1,0,2:T(4,128)S(1)} %get-tuple-element.61), channel_id=1, source_target_pairs={{0,4},{4,8},{8,12},{1,5},{5,9},{9,13},{2,6},{6,10},{10,14},{3,7},{... | collective-permute-start | bytes 20744 | tf_op jit(solution)/shard_map/ppermute | solution.py:26
  125.7 0.7 collective-permute-start.3
  126.4 0.7 collective-permute-start.4
  127.2 3.4 %collective-permute-start.6 = (f32[144]{0:T(256)S(1)}, f32[144]{0:T(256)S(1)}, u32[]{:S(2)}, u32[]{:S(2)}) collective-permute-start(f32[144]{0:T(256)S(1)} %get-tuple-element.115), channel_id=1, source_target_pairs={{0,4},{4,8},{8,12},{1,5},{5,9},{9,13},{2,6},{6,10},{10,14},{3,7},{... | collective-permute-start | bytes 1736 | tf_op jit(solution)/shard_map/ppermute | solution.py:26
  130.6 0.7 collective-permute-start.7
  131.2 1.1 collective-permute-done.2
  132.3 0.6 collective-permute-start.8
  133.3 0.6 collective-permute-start.5
  134.0 7.6 %collective-permute-done.5 = f32[4,3,144]{1,0,2:T(4,128)S(1)} collective-permute-done((f32[4,3,144]{1,0,2:T(4,128)S(1)}, f32[4,3,144]{1,0,2:T(4,128)S(1)}, u32[]{:S(2)}, u32[]{:S(2)}) %collective-permute-start.5) | collective-permute-done | bytes 6944 | tf_op jit(solution)/shard_map/ppermute | solution.py:16
  141.8 0.8 copy.211
  (121 shorter events, 20.4 us)
Async XLA Ops:
  6.5 44.5 %copy-start = (f32[4,256]{1,0:T(4,128)S(1)}, f32[4,256]{1,0:T(4,128)}, u32[]{:S(2)}) copy-start(f32[4,256]{1,0:T(4,128)} %param.19) | copy-start | bytes 12292
  6.5 24.9 %copy-start.3 = (bf16[27,16,256]{2,1,0:T(8,128)(2,1)S(1)}, bf16[27,16,256]{2,1,0:T(8,128)(2,1)}, u32[]{:S(2)}) copy-start(bf16[27,16,256]{2,1,0:T(8,128)(2,1)} %param.12) | copy-start | bytes 663556
  6.5 73.0 %all-gather.2.cloned.1.call-start = ((), (), s32[]{:S(2)}) async-start(), calls=%async_computation | async-start | bytes 2359296 | tf_op jit(solution)/shard_map/all_gather | solution.py:145
  29.1 2.1 %collective-permute-start = (bf16[2,16,256]{2,1,0:T(8,128)(2,1)S(1)}, bf16[2,16,256]{2,1,0:T(8,128)(2,1)S(1)}, u32[]{:S(2)}, u32[]{:S(2)}) collective-permute-start(bf16[2,16,256]{2,1,0:T(8,128)(2,1)S(1)} %slice.742), channel_id=1, source_target_pairs={{0,1},{2,3},{4,5},{6,7},{8,9},{10,11},{12,13},{14,15},{16,17},{18,... | collective-permute-start | bytes 49160 | tf_op jit(solution)/shard_map/ppermute | solution.py:26
  42.2 4.1 %copy-start.4 = (f32[256]{0:T(256)S(1)}, f32[256]{0:T(256)}, u32[]{:S(2)}) copy-start(f32[256]{0:T(256)} %param.14) | copy-start | bytes 3076
  42.2 4.0 %copy-start.5 = (f32[256]{0:T(256)S(1)}, f32[256]{0:T(256)}, u32[]{:S(2)}) copy-start(f32[256]{0:T(256)} %param.13) | copy-start | bytes 3076
  46.6 3.4 %collective-permute-start.1 = (bf16[2,256,256]{1,2,0:T(8,128)(2,1)S(1)}, bf16[2,256,256]{1,2,0:T(8,128)(2,1)S(1)}, u32[]{:S(2)}, u32[]{:S(2)}) collective-permute-start(bf16[2,256,256]{1,2,0:T(8,128)(2,1)S(1)} %slice.825), channel_id=1, source_target_pairs={{0,1},{2,3},{4,5},{6,7},{8,9},{10,11},{12,13},{14,15},{16,17},{18,... | collective-permute-start | bytes 786440 | tf_op jit(solution)/shard_map/ppermute | solution.py:26
  79.5 4.3 %copy-start.2 = (bf16[6,512,256]{1,2,0:T(8,128)(2,1)S(1)}, bf16[6,512,256]{1,2,0:T(8,128)(2,1)}, u32[]{:S(2)}) copy-start(bf16[6,512,256]{1,2,0:T(8,128)(2,1)} %all-gather.2.cloned.1.call-done) | copy-start | bytes 4718596
  93.5 6.1 %slice-start = ((s8[7077888]{0:T(1024)(128)(4,1)}), s8[4194304]{0:T(1024)(128)(4,1)S(1)}, s32[]{:S(2)}) async-start(s8[7077888]{0:T(1024)(128)(4,1)} %bitcast.319), calls=%async_computation.1 | async-start | bytes 8388608
  96.5 3.0 %slice-start.1 = ((s8[7077888]{0:T(1024)(128)(4,1)}), s8[2883584]{0:T(1024)(128)(4,1)S(1)}, s32[]{:S(2)}) async-start(s8[7077888]{0:T(1024)(128)(4,1)} %bitcast.319), calls=%async_computation.2 | async-start | bytes 5767168
  108.3 3.8 %copy-start.6 = (bf16[3,256]{1,0:T(4,128)(2,1)S(1)}, bf16[3,256]{1,0:T(4,128)(2,1)}, u32[]{:S(2)}) copy-start(bf16[3,256]{1,0:T(4,128)(2,1)} %param.18) | copy-start | bytes 4612
  108.4 3.8 %copy-start.7 = (f32[256]{0:T(256)S(1)}, f32[256]{0:T(256)}, u32[]{:S(2)}) copy-start(f32[256]{0:T(256)} %param.17) | copy-start | bytes 3076
  108.4 3.8 %copy-start.8 = (f32[256]{0:T(256)S(1)}, f32[256]{0:T(256)}, u32[]{:S(2)}) copy-start(f32[256]{0:T(256)} %param.16) | copy-start | bytes 3076
  121.6 21.0 %copy-start.1 = (f32[4,256]{1,0:T(4,128)S(1)}, f32[4,256]{1,0:T(4,128)}, u32[]{:S(2)}) copy-start(f32[4,256]{1,0:T(4,128)} %param.19) | copy-start | bytes 12292
  122.3 10.0 %collective-permute-start.2 = (f32[4,3,144]{1,0,2:T(4,128)S(1)}, f32[4,3,144]{1,0,2:T(4,128)S(1)}, u32[]{:S(2)}, u32[]{:S(2)}) collective-permute-start(f32[4,3,144]{1,0,2:T(4,128)S(1)} %get-tuple-element.61), channel_id=1, source_target_pairs={{0,4},{4,8},{8,12},{1,5},{5,9},{9,13},{2,6},{6,10},{10,14},{3,7},{... | collective-permute-start | bytes 20744 | tf_op jit(solution)/shard_map/ppermute | solution.py:26
  125.7 7.2 %collective-permute-start.3 = (f32[4,3,144]{1,0,2:T(4,128)S(1)}, f32[4,3,144]{1,0,2:T(4,128)S(1)}, u32[]{:S(2)}, u32[]{:S(2)}) collective-permute-start(f32[4,3,144]{1,0,2:T(4,128)S(1)} %get-tuple-element.62), channel_id=1, source_target_pairs={} | collective-permute-start | bytes 20744 | tf_op jit(solution)/shard_map/ppermute | solution.py:26
  126.4 6.6 %collective-permute-start.4 = (f32[4,3,144]{1,0,2:T(4,128)S(1)}, f32[4,3,144]{1,0,2:T(4,128)S(1)}, u32[]{:S(2)}, u32[]{:S(2)}) collective-permute-start(f32[4,3,144]{1,0,2:T(4,128)S(1)} %get-tuple-element.63), channel_id=1, source_target_pairs={} | collective-permute-start | bytes 20744 | tf_op jit(solution)/shard_map/ppermute | solution.py:26
  127.2 6.7 %collective-permute-start.6 = (f32[144]{0:T(256)S(1)}, f32[144]{0:T(256)S(1)}, u32[]{:S(2)}, u32[]{:S(2)}) collective-permute-start(f32[144]{0:T(256)S(1)} %get-tuple-element.115), channel_id=1, source_target_pairs={{0,4},{4,8},{8,12},{1,5},{5,9},{9,13},{2,6},{6,10},{10,14},{3,7},{... | collective-permute-start | bytes 1736 | tf_op jit(solution)/shard_map/ppermute | solution.py:26
  130.6 3.3 %collective-permute-start.7 = (f32[144]{0:T(256)S(1)}, f32[144]{0:T(256)S(1)}, u32[]{:S(2)}, u32[]{:S(2)}) collective-permute-start(f32[144]{0:T(256)S(1)} %get-tuple-element.116), channel_id=1, source_target_pairs={} | collective-permute-start | bytes 1736 | tf_op jit(solution)/shard_map/ppermute | solution.py:26
  132.3 1.6 %collective-permute-start.8 = (f32[144]{0:T(256)S(1)}, f32[144]{0:T(256)S(1)}, u32[]{:S(2)}, u32[]{:S(2)}) collective-permute-start(f32[144]{0:T(256)S(1)} %get-tuple-element.117), channel_id=1, source_target_pairs={} | collective-permute-start | bytes 1736 | tf_op jit(solution)/shard_map/ppermute | solution.py:26
  133.3 8.3 %collective-permute-start.5 = (f32[4,3,144]{1,0,2:T(4,128)S(1)}, f32[4,3,144]{1,0,2:T(4,128)S(1)}, u32[]{:S(2)}, u32[]{:S(2)}) collective-permute-start(f32[4,3,144]{1,0,2:T(4,128)S(1)} %fusion.128), channel_id=1, source_target_pairs={{0,2},{2,0},{1,3},{3,1},{4,6},{6,4},{5,7},{7,5},{8,10},{10,8},{9,1... | collective-permute-start | bytes 20744 | tf_op jit(solution)/shard_map/ppermute | solution.py:16
Sparse Core Ops, SparseCore 0:
  51.1 28.3 all-gather.1
